TPU v7x, 32 devices: a whole 2x2x4 slice. The times are simulated.
32 devices in a mesh: layer: 2 (over y), feat: 4 (over x, core), width: 4 (over z).
Axes of the slice: x: 2, y: 2, z: 4, core: 2. Of those that a mesh axis runs over, the one named last changes fastest.
Arguments:
- resid: bfloat16 [2, 128, 2048], P(None, 'layer', 'width'), may hold values from -6 to 6
- enc_w: bfloat16 [2, 2048, 65536], P(None, 'width', ('layer', 'feat')), may hold values from -0.125 to 0.125
- enc_b: float32 [2, 65536], P(None, ('layer', 'feat')), may hold values from -3 to 3
- dec_w: float32 [3, 65536, 2048], P(None, ('layer', 'feat'), 'width'), may hold values from -0.03125 to 0.03125
- dec_b: float32 [2, 2048], P(None, 'width'), may hold values from -2 to 2
- target: float32 [2, 128, 2048], P(None, ('layer', 'feat'), 'width'), may hold values from -6 to 6
Outputs:
- recon: float32 [2, 128, 2048], P(None, ('layer', 'feat'), 'width')
- err: float32 [2, 128], P(None, ('layer', 'feat'))
All inputs are finite; a program needn't handle non-finite values.
Results may differ from a plain program's by a relative error of at most 0.00035.
Values may be sent and summed in bfloat16 or wider, within the bound.
No kernel may reach another device: no remote copies, remote signals or barrier semaphores. Data moves between devices by JAX's collectives and lax.ppermute only.
A program may use at most 128 MiB of HBM per device.

v0:
```python
import jax
import jax.numpy as jnp
from jax import lax
from jax.sharding import PartitionSpec as P


def decode_rows(act, dec_w, target_idx):
    total = None
    for layer_idx in range(target_idx + 1):
        block = target_idx * (target_idx + 1) // 2 + layer_idx
        rows = act[layer_idx]
        term = jnp.dot(
            rows, dec_w[block], precision=lax.Precision.HIGHEST, preferred_element_type=jnp.float32
        )
        total = term if total is None else total + term
    return total


def per_device(resid, enc_w, enc_b, dec_w, dec_b, target):
    layers = resid.shape[0]
    gathered = lax.all_gather(resid, "layer", axis=1, tiled=True)
    tokens = gathered.shape[1]
    partial_pre = jnp.einsum("ltd,ldf->ltf", gathered, enc_w, preferred_element_type=jnp.float32)
    pre = lax.psum(partial_pre, "width")
    act = jnp.maximum(pre + enc_b[:, None, :], 0.0)
    own_rows = tokens // lax.axis_size(("layer", "feat"))
    summed = lax.psum_scatter(
        jnp.concatenate(
            [decode_rows(act, dec_w, target_idx) for target_idx in range(layers)], axis=1
        ),
        ("layer", "feat"),
        scatter_dimension=0,
        tiled=True,
    )
    summed = summed.reshape(own_rows, layers, dec_w.shape[2]).transpose(1, 0, 2)
    recon = summed + dec_b[:, None, :]
    diff = recon - target
    sq_error, sq_target = lax.psum(
        (jnp.sum(diff * diff, axis=2), jnp.sum(target * target, axis=2)), "width"
    )
    err = sq_error / (sq_target + 1e-06)
    return (recon, err)


def solution(mesh):
    in_specs = (
        P(None, "layer", "width"),
        P(None, "width", ("layer", "feat")),
        P(None, ("layer", "feat")),
        P(None, ("layer", "feat"), "width"),
        P(None, "width"),
        P(None, ("layer", "feat"), "width"),
    )
    out_specs = (P(None, ("layer", "feat"), "width"), P(None, ("layer", "feat")))
    return jax.shard_map(
        per_device, mesh=mesh, in_specs=in_specs, out_specs=out_specs, check_vma=False
    )
```

profile of v0, /device:TPU:0, one launch (start us, length us, event | category | flops | bytes accessed | tf_op | source)
XLA Modules:
  0.0 413.2 jit_solution(15221711624656479680)
XLA Ops:
  7.2 0.0 all-reduce.3.cloned.1.call-start
  7.2 7.4 %all_gather.3 = bf16[2,128,512]{2,1,0:T(8,128)(2,1)S(1)} all-gather(bf16[2,64,512]{2,1,0:T(8,128)(2,1)} %param.6), channel_id=1, replica_groups=mesh['layer'=2,'feat'=4,'width'=4] {'layer'}, dimensions={1}, use_global_device_ids=true | all-gather | bytes 393216 | tf_op jit(solution)/shard_map/all_gather | solution.py:21
  14.6 11.3 %fusion.14 = f32[2,128,8192]{2,1,0:T(8,128)} fusion(bf16[2,128,512]{2,1,0:T(8,128)(2,1)S(1)} %all_gather.3, bf16[2,512,8192]{2,1,0:T(8,128)(2,1)} %param.7), kind=kOutput, calls=%fused_computation.19 | convolution fusion | flops 2147483648 | bytes 25427968 | tf_op jit(solution)/shard_map/ltd,ldf->ltf/dot_general | solution.py:23
  26.0 0.0 copy-start
  26.0 0.0 all-reduce.3.cloned.1.call-update
  26.0 0.0 reduce-scatter.2.cloned.1.call-start
  26.0 292.4 %all-reduce.3.cloned.1.call-done = f32[2,128,8192]{2,1,0:T(8,128)} async-done(((f32[2,128,8192]{2,1,0:T(8,128)}), f32[2,128,8192]{2,1,0:T(8,128)}) %all-reduce.3.cloned.1.call-update) | async-done | bytes 8388624 | tf_op jit(solution)/shard_map/psum | solution.py:24
  318.4 0.0 copy-done
  318.4 4.2 %add_maximum_fusion = f32[2,128,8192]{2,1,0:T(8,128)S(1)} fusion(f32[2,128,8192]{2,1,0:T(8,128)} %all-reduce.3.cloned.1.call-done, f32[2,8192]{1,0:T(2,128)S(1)} %copy-done), kind=kLoop, calls=%fused_computation.9 | loop fusion | flops 4194304 | bytes 16842752 | tf_op jit(solution)/shard_map/max | solution.py:25
  322.6 11.9 %fusion = f32[128,512]{1,0:T(8,128)S(1)} fusion(f32[3,8192,512]{2,1,0:T(8,128)} %param.9, f32[2,128,8192]{2,1,0:T(8,128)S(1)} %add_maximum_fusion), kind=kOutput, calls=%fused_computation | convolution fusion | flops 6442450944 | bytes 21233664 | tf_op jit(solution)/shard_map/dot_general | solution.py:12
  334.5 11.9 %fusion.4 = f32[128,512]{1,0:T(8,128)S(1)} fusion(f32[3,8192,512]{2,1,0:T(8,128)} %param.9, f32[2,128,8192]{2,1,0:T(8,128)S(1)} %add_maximum_fusion), kind=kOutput, calls=%fused_computation.4 | convolution fusion | flops 6442450944 | bytes 21233664 | tf_op jit(solution)/shard_map/dot_general | solution.py:12
  346.4 0.0 copy-start.1
  346.4 0.0 copy-start.2
  346.4 12.1 %fusion.9 = f32[128,512]{1,0:T(8,128)S(1)} fusion(f32[128,512]{1,0:T(8,128)S(1)} %fusion, f32[3,8192,512]{2,1,0:T(8,128)} %param.9, f32[2,128,8192]{2,1,0:T(8,128)S(1)} %add_maximum_fusion), kind=kOutput, calls=%fused_computation.12 | convolution fusion | flops 6442516480 | bytes 21495808 | tf_op jit(solution)/shard_map/dot_general | solution.py:12
  358.5 0.8 pad_maximum_fusion
  359.3 0.0 reduce-scatter.2.cloned.1.call-update
  359.4 33.2 %reduce-scatter.2.cloned.1.call-done = f32[16,1024]{1,0:T(8,128)} async-done(((f32[128,1024]{1,0:T(8,128)}), f32[16,1024]{1,0:T(8,128)}) %reduce-scatter.2.cloned.1.call-update) | async-done | bytes 65552 | tf_op jit(solution)/shard_map/reduce_scatter | solution.py:27
  392.6 0.0 copy-done.1
  392.6 0.0 copy-done.2
  392.6 1.5 multiply_reduce_fusion
  394.1 11.6 %all-reduce = (f32[2,16]{1,0:T(2,128)S(1)}, f32[2,16]{1,0:T(2,128)S(1)}) all-reduce(f32[2,16]{1,0:T(2,128)S(1)} %get-tuple-element.3, f32[2,16]{1,0:T(2,128)S(1)} %get-tuple-element.2), channel_id=1, replica_groups=mesh['layer'=2,'feat'=4,'width'=4] {'width'}, use_global_device_ids=true, to_apply=%region_3.0 | all-reduce | flops 64 | bytes 512 | tf_op jit(solution)/shard_map/psum | solution.py:38
  405.8 0.6 add_divide_fusion
Async XLA Ops:
  7.2 311.2 %all-reduce.3.cloned.1.call-start = ((), (), s32[]{:S(2)}) async-start(), calls=%async_computation.1 | async-start | bytes 16777216 | tf_op jit(solution)/shard_map/psum | solution.py:24
  26.0 292.4 %copy-start = (f32[2,8192]{1,0:T(2,128)S(1)}, f32[2,8192]{1,0:T(2,128)}, u32[]{:S(2)}) copy-start(f32[2,8192]{1,0:T(2,128)} %param.8) | copy-start | bytes 196612
  26.0 366.6 %reduce-scatter.2.cloned.1.call-start = ((), (), s32[]{:S(2)}) async-start(), calls=%async_computation.2 | async-start | bytes 589824 | tf_op jit(solution)/shard_map/reduce_scatter | solution.py:27
  346.4 46.2 %copy-start.1 = (f32[2,16,512]{2,1,0:T(8,128)S(1)}, f32[2,16,512]{2,1,0:T(8,128)}, u32[]{:S(2)}) copy-start(f32[2,16,512]{2,1,0:T(8,128)} %param.11) | copy-start | bytes 196612
  346.4 46.2 %copy-start.2 = (f32[2,512]{1,0:T(2,128)S(1)}, f32[2,512]{1,0:T(2,128)}, u32[]{:S(2)}) copy-start(f32[2,512]{1,0:T(2,128)} %param.10) | copy-start | bytes 12292
Sparse Core Ops, SparseCore 0:
  26.1 292.2 all-reduce.2
  359.5 33.0 reduce-scatter.1
where the time goes:
time: 413 us
  waiting for transfers between devices  326 us (79%)
  matrix products  47.2 us (11%)
  blocking collectives  19.1 us (5%)
  between operations  14.1 us (3%)
  other arithmetic  7.07 us (2%)
    psum x1, waiting for transfers between devices, per_device(): pre = lax.psum(partial_pre, 'width')  292 us
    dot_general x3, matrix products, decode_rows(): jnp.dot(rows, dec_w[block], precision=lax.Precision.HIGHEST, preferred_el...  35.9 us
    reduce_scatter x1, waiting for transfers between devices, per_device(): lax.psum_scatter(jnp.concatenate([decode_rows(act, dec_w, target_idx) for...  33.2 us
    psum x1, blocking collectives, per_device(): lax.psum((jnp.sum(diff * diff, axis=2), jnp.sum(target * target, axis=2))...  11.6 us
    dot_general x1, matrix products, per_device(): jnp.einsum('ltd,ldf->ltf', gathered, enc_w, preferred_element_type=jnp.fl...  11.3 us
  transfers between devices with their start and end apart: 2, of which 2 were waited for; matrix products, arithmetic and copies ran while one was open for 0% of the time, Pallas kernels for 0%

commit v1 on v0

--- a/solution.py
+++ b/solution.py
@@ -21,7 +21,7 @@
     gathered = lax.all_gather(resid, "layer", axis=1, tiled=True)
     tokens = gathered.shape[1]
     partial_pre = jnp.einsum("ltd,ldf->ltf", gathered, enc_w, preferred_element_type=jnp.float32)
-    pre = lax.psum(partial_pre, "width")
+    pre = lax.all_gather(partial_pre, "width").sum(axis=0)
     act = jnp.maximum(pre + enc_b[:, None, :], 0.0)
     own_rows = tokens // lax.axis_size(("layer", "feat"))
     summed = lax.psum_scatter(

time: 413 us -> 699 us (1.69)
  waiting for transfers between devices: 326 us -> 595 us
  other arithmetic: 7.07 us -> 22.7 us
    all_gather x0 -> x1, waiting for transfers between devices: none -> 563 us  [per_device(): pre = lax.all_gather(partial_pre, 'width').sum(axis=0)]
    psum x1 -> x0, waiting for transfers between devices: 292 us -> none  [per_device(): pre = lax.psum(partial_pre, 'width')]
    reduce_sum x0 -> x1, other arithmetic: none -> 15.7 us  [per_device(): pre = lax.all_gather(partial_pre, 'width').sum(axis=0)]
where the time goes in v1:
time: 699 us
  waiting for transfers between devices  595 us (85%)
  matrix products  47.2 us (7%)
  other arithmetic  22.7 us (3%)
  blocking collectives  19.1 us (3%)
  between operations  14.1 us (2%)
    all_gather x1, waiting for transfers between devices, per_device(): pre = lax.all_gather(partial_pre, 'width').sum(axis=0)  563 us
    dot_general x3, matrix products, decode_rows(): jnp.dot(rows, dec_w[block], precision=lax.Precision.HIGHEST, preferred_el...  35.9 us
    reduce_scatter x1, waiting for transfers between devices, per_device(): lax.psum_scatter(jnp.concatenate([decode_rows(act, dec_w, target_idx) for...  32.5 us
    reduce_sum x1, other arithmetic, per_device(): pre = lax.all_gather(partial_pre, 'width').sum(axis=0)  15.7 us
  transfers between devices with their start and end apart: 2, of which 2 were waited for; matrix products, arithmetic and copies ran while one was open for 0% of the time, Pallas kernels for 0%

profile of v1, /device:TPU:0, one launch (start us, length us, event | category | flops | bytes accessed | tf_op | source)
XLA Modules:
  0.0 698.6 jit_solution(2223347936660237197)
XLA Ops:
  7.2 0.0 all-gather.3.cloned.1.call-start
  7.2 7.4 %all_gather.9 = bf16[2,128,512]{2,1,0:T(8,128)(2,1)S(1)} all-gather(bf16[2,64,512]{2,1,0:T(8,128)(2,1)} %param.6), channel_id=1, replica_groups=mesh['layer'=2,'feat'=4,'width'=4] {'layer'}, dimensions={1}, use_global_device_ids=true | all-gather | bytes 393216 | tf_op jit(solution)/shard_map/all_gather | solution.py:21
  14.6 11.3 %fusion.14 = f32[2,128,8192]{2,1,0:T(8,128)} fusion(bf16[2,128,512]{2,1,0:T(8,128)(2,1)S(1)} %all_gather.9, bf16[2,512,8192]{2,1,0:T(8,128)(2,1)} %param.7), kind=kOutput, calls=%fused_computation.19 | convolution fusion | flops 2147483648 | bytes 25427968 | tf_op jit(solution)/shard_map/ltd,ldf->ltf/dot_general | solution.py:23
  26.0 0.0 all-gather.3.cloned.1.call-update
  26.0 0.2 reduce-scatter.2.cloned.1.call-start
  26.2 562.7 %all-gather.3.cloned.1.call-done = f32[8,128,8192]{2,1,0:T(8,128)} async-done(((f32[2,128,8192]{2,1,0:T(8,128)}), f32[8,128,8192]{2,1,0:T(8,128)}) %all-gather.3.cloned.1.call-update) | async-done | bytes 33554448 | tf_op jit(solution)/shard_map/all_gather | solution.py:24
  588.9 0.0 copy-start
  588.9 15.7 %reduce_sum.27 = f32[2,128,8192]{2,1,0:T(8,128)} reduce(f32[4,2,128,8192]{3,2,1,0:T(8,128)} %bitcast.32, f32[]{:T(128)} %constant.2.clone.1), dimensions={0}, to_apply=%region_0.0 | reduce | flops 6291456 | bytes 41943044 | tf_op jit(solution)/shard_map/reduce_sum | solution.py:24
  604.6 0.0 copy-done
  604.6 4.2 add_maximum_fusion
  608.8 11.9 %fusion = f32[128,512]{1,0:T(8,128)S(1)} fusion(f32[3,8192,512]{2,1,0:T(8,128)} %param.9, f32[2,128,8192]{2,1,0:T(8,128)S(1)} %add_maximum_fusion), kind=kOutput, calls=%fused_computation | convolution fusion | flops 6442450944 | bytes 21233664 | tf_op jit(solution)/shard_map/dot_general | solution.py:12
  620.7 11.9 %fusion.4 = f32[128,512]{1,0:T(8,128)S(1)} fusion(f32[3,8192,512]{2,1,0:T(8,128)} %param.9, f32[2,128,8192]{2,1,0:T(8,128)S(1)} %add_maximum_fusion), kind=kOutput, calls=%fused_computation.4 | convolution fusion | flops 6442450944 | bytes 21233664 | tf_op jit(solution)/shard_map/dot_general | solution.py:12
  632.6 0.0 copy-start.1
  632.6 0.0 copy-start.2
  632.6 12.1 %fusion.9 = f32[128,512]{1,0:T(8,128)S(1)} fusion(f32[128,512]{1,0:T(8,128)S(1)} %fusion, f32[3,8192,512]{2,1,0:T(8,128)} %param.9, f32[2,128,8192]{2,1,0:T(8,128)S(1)} %add_maximum_fusion), kind=kOutput, calls=%fused_computation.12 | convolution fusion | flops 6442516480 | bytes 21495808 | tf_op jit(solution)/shard_map/dot_general | solution.py:12
  644.8 0.8 pad_maximum_fusion
  645.6 0.0 reduce-scatter.2.cloned.1.call-update
  645.6 32.5 %reduce-scatter.2.cloned.1.call-done = f32[16,1024]{1,0:T(8,128)} async-done(((f32[128,1024]{1,0:T(8,128)}), f32[16,1024]{1,0:T(8,128)}) %reduce-scatter.2.cloned.1.call-update) | async-done | bytes 65552 | tf_op jit(solution)/shard_map/reduce_scatter | solution.py:27
  678.1 0.0 copy-done.1
  678.1 0.0 copy-done.2
  678.1 1.5 multiply_reduce_fusion
  679.6 11.6 %all-reduce = (f32[2,16]{1,0:T(2,128)S(1)}, f32[2,16]{1,0:T(2,128)S(1)}) all-reduce(f32[2,16]{1,0:T(2,128)S(1)} %get-tuple-element.3, f32[2,16]{1,0:T(2,128)S(1)} %get-tuple-element.2), channel_id=1, replica_groups=mesh['layer'=2,'feat'=4,'width'=4] {'width'}, use_global_device_ids=true, to_apply=%region_3.0 | all-reduce | flops 64 | bytes 512 | tf_op jit(solution)/shard_map/psum | solution.py:38
  691.2 0.6 add_divide_fusion
Async XLA Ops:
  7.2 581.8 %all-gather.3.cloned.1.call-start = ((), (), s32[]{:S(2)}) async-start(), calls=%async_computation.2 | async-start | bytes 41943040 | tf_op jit(solution)/shard_map/all_gather | solution.py:24
  26.0 652.1 %reduce-scatter.2.cloned.1.call-start = ((), (), s32[]{:S(2)}) async-start(), calls=%async_computation.1 | async-start | bytes 589824 | tf_op jit(solution)/shard_map/reduce_scatter | solution.py:27
  588.9 15.7 %copy-start = (f32[2,8192]{1,0:T(2,128)S(1)}, f32[2,8192]{1,0:T(2,128)}, u32[]{:S(2)}) copy-start(f32[2,8192]{1,0:T(2,128)} %param.8) | copy-start | bytes 196612
  632.6 45.5 %copy-start.1 = (f32[2,16,512]{2,1,0:T(8,128)S(1)}, f32[2,16,512]{2,1,0:T(8,128)}, u32[]{:S(2)}) copy-start(f32[2,16,512]{2,1,0:T(8,128)} %param.11) | copy-start | bytes 196612
  632.6 45.5 %copy-start.2 = (f32[2,512]{1,0:T(2,128)S(1)}, f32[2,512]{1,0:T(2,128)}, u32[]{:S(2)}) copy-start(f32[2,512]{1,0:T(2,128)} %param.10) | copy-start | bytes 12292
Sparse Core Ops, SparseCore 0:
  26.1 562.7 all-gather.2
  645.7 32.2 reduce-scatter.1
